TPU v7x, 256 devices: a whole 4x4x8 slice. The times are simulated.
256 devices in a mesh: dp: 8 (over z), tensor: 32 (over x, y, core).
Axes of the slice: x: 4, y: 4, z: 8, core: 2. Of those that a mesh axis runs over, the one named last changes fastest.
Arguments:
- hidden: bfloat16 [16384, 2048], P(('dp', 'tensor')), may hold values from -190 to 190
- norm_gain: float32 [2048], replicated, may hold values from 0.1 to 1.9
- head_weight: bfloat16 [2048, 50304], P(None, 'tensor'), may hold values from -0.3 to 0.3
- value_weight: bfloat16 [2048], replicated, may hold values from -0.125 to 0.125
- token_ids: int32 [16384], P(('dp', 'tensor')), may hold values from 0 to 50303
- slot_mask: int32 [16384], P(('dp', 'tensor')), may hold values from 0 to 1, as said below
- lengths: int32 [8, 8], P('dp'), may hold values from 1 to 512, 2048 in all within a row
- request_order: int32 [64], P('dp'), may hold values from 0 to 63, each once
Outputs:
- token_logprob: float32 [16384], P(('dp', 'tensor'))
- token_entropy: float32 [16384], P(('dp', 'tensor'))
- token_value: float32 [16384], P(('dp', 'tensor'))
- request_score: float32 [64], P('dp')
Inputs may be any that keep to these rules, and one draw needn't show every extreme that they name: `slot_mask`: 0 or 1. Among the 64 slots of one device at most 48 are 1 and at least half of 48, rounded down; in every draw some device has exactly 48.
All inputs are finite; a program needn't handle non-finite values.
Results may differ from a plain program's by a relative error of at most 0.0029.
Values may be sent and summed in bfloat16 or wider, within the bound.
A program may use at most 64 MiB of HBM per device.

v0:
```python
import jax
import jax.numpy as jnp
from jax import lax
from jax.sharding import PartitionSpec as P

EPSILON = 1e-06


def merged_2(value, axis, join):
    pieces = jax.tree.map(lambda part: lax.all_gather(part, axis), value)
    head = jax.tree.map(lambda part: part[0], pieces)
    tail = jax.tree.map(lambda part: part[1:], pieces)
    subtotal, _ = lax.scan(lambda subtotal, share: (join(subtotal, share), None), head, tail)
    return subtotal


def combine_parts(lhs_part, rhs_part):
    row_peak = jnp.maximum(lhs_part[0], rhs_part[0])
    left_factor = jnp.exp(lhs_part[0] - row_peak)
    right_factor = jnp.exp(rhs_part[0] - row_peak)
    row_mass = left_factor * lhs_part[1] + right_factor * rhs_part[1]
    row_spread = left_factor * (
        lhs_part[2] + (lhs_part[0] - row_peak) * lhs_part[1]
    ) + right_factor * (rhs_part[2] + (rhs_part[0] - row_peak) * rhs_part[1])
    return (row_peak, row_mass, row_spread, lhs_part[3] + rhs_part[3])


def on_device(
    hidden, norm_gain, head_weight, value_weight, token_ids, slot_mask, lengths, request_order
):
    own_rows = hidden.shape[0]
    vocab_local = head_weight.shape[1]
    tensor_index = lax.axis_index("tensor")
    widened = hidden.astype(jnp.float32)
    inverse_rms = lax.rsqrt(jnp.mean(widened * widened, axis=1, keepdims=True) + EPSILON)
    normed = (widened * inverse_rms * norm_gain).astype(jnp.bfloat16)
    weight_mask = slot_mask.astype(jnp.float32)
    token_value = weight_mask * jnp.dot(normed, value_weight, preferred_element_type=jnp.float32)
    sent_count = normed.shape[0]
    columns = tensor_index * vocab_local + jnp.arange(vocab_local, dtype=jnp.int32)
    piece_rows = lax.all_gather(normed, "tensor", axis=0, tiled=True)
    piece_ids = lax.all_gather(token_ids, "tensor", axis=0, tiled=True)
    logits = jnp.dot(piece_rows, head_weight, preferred_element_type=jnp.float32)
    row_peak = jnp.max(logits, axis=1)
    shifted = logits - row_peak[:, None]
    weights = jnp.exp(shifted)
    row_mass = jnp.sum(weights, axis=1)
    row_spread = jnp.sum(weights * shifted, axis=1)
    row_target = jnp.sum(jnp.where(columns[None, :] == piece_ids[:, None], logits, 0.0), axis=1)
    updates = (row_peak, row_mass, row_spread, row_target)
    row_peak, row_mass, row_spread, row_target = tuple((update for update in updates))
    own_start = tensor_index * sent_count
    merged = merged_2((row_peak, row_mass, row_spread, row_target), "tensor", combine_parts)
    row_peak, row_mass, row_spread, row_target = [
        lax.dynamic_slice_in_dim(member, own_start, sent_count) for member in merged
    ]
    log_mass = jnp.log(row_mass)
    token_logprob = weight_mask * (row_target - row_peak - log_mass)
    token_entropy = weight_mask * (log_mass - row_spread / row_mass)
    request_count = lengths.shape[1]
    span_lengths = lengths[0]
    span_ends = jnp.cumsum(span_lengths)
    slot_ids = tensor_index * own_rows + jnp.arange(own_rows, dtype=jnp.int32)
    position = jnp.sum((slot_ids[:, None] >= span_ends[None, :]).astype(jnp.int32), axis=1)
    onehot = position[:, None] == jnp.arange(request_count, dtype=jnp.int32)[None, :]
    by_pos = jnp.sum(jnp.where(onehot, token_logprob[:, None], 0.0), axis=0) / span_lengths.astype(
        jnp.float32
    )
    all_requests = request_count * lax.axis_size("dp")
    route_table = request_order[:, None] == jnp.arange(all_requests, dtype=jnp.int32)[None, :]
    by_request = jnp.sum(jnp.where(route_table, by_pos[:, None], 0.0), axis=0)
    totals = lax.psum(by_request, ("dp", "tensor"))
    request_score = lax.dynamic_slice_in_dim(
        totals, lax.axis_index("dp") * request_count, request_count
    )
    return (token_logprob, token_entropy, token_value, request_score)


def solution(mesh):
    return jax.shard_map(
        on_device,
        mesh=mesh,
        in_specs=(
            P(("dp", "tensor"), None),
            P(),
            P(None, "tensor"),
            P(),
            P(("dp", "tensor")),
            P(("dp", "tensor")),
            P("dp", None),
            P("dp"),
        ),
        out_specs=(P(("dp", "tensor")), P(("dp", "tensor")), P(("dp", "tensor")), P("dp")),
        check_vma=False,
    )
```

profile of v0, /device:TPU:1, one launch (start us, length us, event | category | flops | bytes accessed | tf_op | source)
XLA Modules:
  0.0 278.3 jit_solution(18414183828398171453)
XLA Ops:
  7.2 0.0 all-gather.6.cloned.1.call-start
  7.2 1.1 fusion.2
  8.3 1.8 fusion.4
  10.1 0.0 all-gather.6.cloned.1.call-update
  10.2 0.8 reduce-window.8
  11.0 0.7 reshape.86
  11.7 1.3 dynamic-slice
  13.6 0.9 dynamic-update-slice
  14.5 14.7 %all-reduce = s32[2048]{0:T(1024)S(1)} all-reduce(s32[2048]{0:T(1024)S(1)} %dynamic-update-slice), channel_id=1, replica_groups=mesh['dp'=8,'tensor'=32] {'tensor'}, use_global_device_ids=true, to_apply=%add | all-reduce | flops 2048 | bytes 16384
  29.2 0.1 convert_reduce_fusion
  29.3 1.6 fusion.1
  30.9 41.9 %all-gather.6.cloned.1.call-done = bf16[2048,2048]{1,0:T(8,128)(2,1)} async-done(((bf16[64,2048]{1,0:T(8,128)(2,1)}), bf16[2048,2048]{1,0:T(8,128)(2,1)}) %all-gather.6.cloned.1.call-update) | async-done | bytes 8388624 | tf_op jit(solution)/shard_map/all_gather | solution.py:41
  72.9 18.4 %fusion.5 = (f32[2048]{0:T(1024)S(1)}, f32[2048,1572]{0,1:T(8,128)S(1)}) fusion(bf16[2048,2048]{1,0:T(8,128)(2,1)} %all-gather.6.cloned.1.call-done, bf16[2048,1572]{0,1:T(8,128)(2,1)} %param.12), kind=kOutput, calls=%fused_computation.28 | convolution fusion | flops 13190109184 | bytes 27713536 | tf_op jit(solution)/shard_map/dot_general | solution.py:43
  91.3 0.0 copy-start
  91.3 0.0 copy-start.2
  91.3 0.0 copy-start.3
  91.3 4.7 %fusion = (f32[2048]{0:T(1024)S(1)}, f32[2048]{0:T(1024)S(1)}, f32[2048]{0:T(1024)S(1)}) fusion(f32[2048,1572]{0,1:T(8,128)S(1)} %get-tuple-element.88, f32[2048]{0:T(1024)S(1)} %get-tuple-element.87, s32[2048]{0:T(1024)S(1)} %all-reduce, s32[1572]{0:T(1024)S(1)} %iota_add_fusion), kind=kLoop, calls=%fused_computation.8 | loop fusion | flops 22530048 | bytes 12925072 | tf_op jit(solution)/shard_map/reduce_sum | solution.py:48
  96.1 24.5 %all-gather.2 = f32[65536]{0:T(1024)S(1)} all-gather(f32[2048]{0:T(1024)S(1)} %get-tuple-element.58), channel_id=4, replica_groups=mesh['dp'=8,'tensor'=32] {'tensor'}, dimensions={0}, use_global_device_ids=true | all-gather | bytes 270336 | tf_op jit(solution)/shard_map/all_gather | solution.py:10
  120.6 22.6 %all-gather = f32[65536]{0:T(1024)S(1)} all-gather(f32[2048]{0:T(1024)S(1)} %get-tuple-element.87), channel_id=2, replica_groups=mesh['dp'=8,'tensor'=32] {'tensor'}, dimensions={0}, use_global_device_ids=true | all-gather | bytes 270336 | tf_op jit(solution)/shard_map/all_gather | solution.py:10
  143.2 24.1 %all-gather.1 = f32[65536]{0:T(1024)S(1)} all-gather(f32[2048]{0:T(1024)S(1)} %get-tuple-element.59), channel_id=3, replica_groups=mesh['dp'=8,'tensor'=32] {'tensor'}, dimensions={0}, use_global_device_ids=true | all-gather | bytes 270336 | tf_op jit(solution)/shard_map/all_gather | solution.py:10
  167.3 22.8 %all-gather.3 = f32[65536]{0:T(1024)S(1)} all-gather(f32[2048]{0:T(1024)S(1)} %get-tuple-element.60), channel_id=5, replica_groups=mesh['dp'=8,'tensor'=32] {'tensor'}, dimensions={0}, use_global_device_ids=true | all-gather | bytes 270336 | tf_op jit(solution)/shard_map/all_gather | solution.py:10
  190.3 4.3 %while.16 = (s32[]{:T(128)}, f32[2048]{0:T(1024)S(1)}, f32[2048]{0:T(1024)S(1)}, f32[2048]{0:T(1024)S(1)}, f32[2048]{0:T(1024)S(1)}, /*index=5*/f32[31,2048]{1,0...) while((s32[]{:T(128)}, f32[2048]{0:T(1024)S(1)}, ...), condition=%wide.region_6.7_spmd, body=%wide.region_5.6_spmd.sunk | while | flops 32770 | bytes 221301 | solution.py:13
  194.6 0.0 copy-done
  194.6 0.6 subtract_multiply_fusion
  195.2 0.0 copy-start.1
  195.2 0.1 select_reduce_fusion.2
  195.3 0.0 copy-done.2
  195.3 0.0 copy-done.3
  195.3 0.1 select_reduce_fusion.1
  195.4 75.4 %psum.7 = f32[64]{0:T(128)S(1)} all-reduce(f32[64]{0:T(128)S(1)} %select_reduce_fusion.1), channel_id=1, replica_groups=mesh['dp'=8,'tensor'=32] {'dp','tensor'}, use_global_device_ids=true, to_apply=%region_11.12 | all-reduce | flops 64 | bytes 512 | tf_op jit(solution)/shard_map/psum | solution.py:72
  270.9 0.6 dynamic_slice.32
  271.5 0.0 copy-done.1
  (203 shorter events, 2.7 us)
Async XLA Ops:
  7.2 65.7 %all-gather.6.cloned.1.call-start = ((), (), s32[]{:S(2)}) async-start(), calls=%async_computation | async-start | bytes 8650752 | tf_op jit(solution)/shard_map/all_gather | solution.py:41
  91.3 103.3 %copy-start = (s32[64]{0:T(128)S(1)}, s32[64]{0:T(128)}, u32[]{:S(2)}) copy-start(s32[64]{0:T(128)} %param.15) | copy-start | bytes 772
  91.3 104.0 %copy-start.2 = (s32[1,8]{1,0:T(1,128)S(1)}, s32[1,8]{1,0:T(1,128)}, u32[]{:S(2)}) copy-start(s32[1,8]{1,0:T(1,128)} %param.16) | copy-start | bytes 100
  91.3 104.0 %copy-start.3 = (s32[8]{0:T(128)S(1)}, s32[8]{0:T(128)}, u32[]{:S(2)}) copy-start(s32[8]{0:T(128)} %param.17) | copy-start | bytes 100
  195.2 76.3 %copy-start.1 = (f32[64]{0:T(128)}, f32[64]{0:T(128)S(1)}, u32[]{:S(2)}) copy-start(f32[64]{0:T(128)S(1)} %get-tuple-element.86) | copy-start | bytes 772
Sparse Core Ops, SparseCore 0:
  10.6 62.2 all-gather.5
where the time goes:
time: 279 us; the launch traced here: 278 us
  blocking collectives  184 us (66%)
  waiting for transfers between devices  42 us (15%)
  matrix products  20.1 us (7%)
  between operations  14.9 us (5%)
  other arithmetic  10.4 us (4%)
  local copies, waits for them, and re-layouts  5.11 us (2%)
    all_gather x4, blocking collectives, merged_2(): pieces = jax.tree.map(lambda part: lax.all_gather(part, axis), value)  93.9 us
    psum x1, blocking collectives, on_device(): totals = lax.psum(by_request, ('dp', 'tensor'))  75.4 us
    all_gather x1, waiting for transfers between devices, on_device(): piece_rows = lax.all_gather(normed, 'tensor', axis=0, tiled=True)  41.9 us
    dot_general x1, matrix products, on_device(): jnp.dot(piece_rows, head_weight, preferred_element_type=jnp.float32)  18.4 us
    unnamed x1, blocking collectives  14.7 us
  transfers between devices with their start and end apart: 1, of which 1 were waited for; matrix products, arithmetic and copies ran while one was open for 2% of the time, Pallas kernels for 0%

commit v1 on v0

--- a/solution.py
+++ b/solution.py
@@ -69,7 +69,7 @@
     all_requests = request_count * lax.axis_size("dp")
     route_table = request_order[:, None] == jnp.arange(all_requests, dtype=jnp.int32)[None, :]
     by_request = jnp.sum(jnp.where(route_table, by_pos[:, None], 0.0), axis=0)
-    totals = lax.psum(by_request, ("dp", "tensor"))
+    totals = lax.psum(lax.psum(by_request, "dp"), "tensor")
     request_score = lax.dynamic_slice_in_dim(
         totals, lax.axis_index("dp") * request_count, request_count
     )

time: 279 us -> 283 us (1.014)
  blocking collectives: 184 us -> 188 us
    psum x1 -> x2, blocking collectives: 75.4 us -> 79.6 us  [on_device(): totals = lax.psum(lax.psum(by_request, 'dp'), 'tensor')]
where the time goes in v1:
time: 283 us; the launch traced here: 282 us
  blocking collectives  188 us (66%)
  waiting for transfers between devices  42 us (15%)
  matrix products  20.1 us (7%)
  between operations  14.9 us (5%)
  other arithmetic  10.4 us (4%)
  local copies, waits for them, and re-layouts  5.11 us (2%)
    all_gather x4, blocking collectives, merged_2(): pieces = jax.tree.map(lambda part: lax.all_gather(part, axis), value)  93.8 us
    psum x2, blocking collectives, on_device(): totals = lax.psum(lax.psum(by_request, 'dp'), 'tensor')  79.6 us
    all_gather x1, waiting for transfers between devices, on_device(): piece_rows = lax.all_gather(normed, 'tensor', axis=0, tiled=True)  41.9 us
    dot_general x1, matrix products, on_device(): jnp.dot(piece_rows, head_weight, preferred_element_type=jnp.float32)  18.4 us
    unnamed x1, blocking collectives  14.7 us
  transfers between devices with their start and end apart: 1, of which 1 were waited for; matrix products, arithmetic and copies ran while one was open for 2% of the time, Pallas kernels for 0%

profile of v1, /device:TPU:1, one launch (start us, length us, event | category | flops | bytes accessed | tf_op | source)
XLA Modules:
  0.0 282.3 jit_solution(14427987406260312339)
XLA Ops:
  7.2 0.0 all-gather.6.cloned.1.call-start
  7.2 1.1 fusion.2
  8.3 1.8 fusion.4
  10.1 0.0 all-gather.6.cloned.1.call-update
  10.2 0.8 reduce-window.8
  11.0 0.7 reshape.86
  11.7 1.3 dynamic-slice
  13.6 0.9 dynamic-update-slice
  14.5 14.7 %all-reduce = s32[2048]{0:T(1024)S(1)} all-reduce(s32[2048]{0:T(1024)S(1)} %dynamic-update-slice), channel_id=1, replica_groups=mesh['dp'=8,'tensor'=32] {'tensor'}, use_global_device_ids=true, to_apply=%add | all-reduce | flops 2048 | bytes 16384
  29.2 0.1 convert_reduce_fusion
  29.3 1.6 fusion.1
  30.9 41.9 %all-gather.6.cloned.1.call-done = bf16[2048,2048]{1,0:T(8,128)(2,1)} async-done(((bf16[64,2048]{1,0:T(8,128)(2,1)}), bf16[2048,2048]{1,0:T(8,128)(2,1)}) %all-gather.6.cloned.1.call-update) | async-done | bytes 8388624 | tf_op jit(solution)/shard_map/all_gather | solution.py:41
  72.9 18.4 %fusion.5 = (f32[2048]{0:T(1024)S(1)}, f32[2048,1572]{0,1:T(8,128)S(1)}) fusion(bf16[2048,2048]{1,0:T(8,128)(2,1)} %all-gather.6.cloned.1.call-done, bf16[2048,1572]{0,1:T(8,128)(2,1)} %param.12), kind=kOutput, calls=%fused_computation.28 | convolution fusion | flops 13190109184 | bytes 27713536 | tf_op jit(solution)/shard_map/dot_general | solution.py:43
  91.3 0.0 copy-start
  91.3 0.0 copy-start.2
  91.3 0.0 copy-start.3
  91.3 4.7 %fusion = (f32[2048]{0:T(1024)S(1)}, f32[2048]{0:T(1024)S(1)}, f32[2048]{0:T(1024)S(1)}) fusion(f32[2048,1572]{0,1:T(8,128)S(1)} %get-tuple-element.88, f32[2048]{0:T(1024)S(1)} %get-tuple-element.87, s32[2048]{0:T(1024)S(1)} %all-reduce, s32[1572]{0:T(1024)S(1)} %iota_add_fusion), kind=kLoop, calls=%fused_computation.8 | loop fusion | flops 22530048 | bytes 12925072 | tf_op jit(solution)/shard_map/reduce_sum | solution.py:48
  96.1 24.5 %all-gather.2 = f32[65536]{0:T(1024)S(1)} all-gather(f32[2048]{0:T(1024)S(1)} %get-tuple-element.58), channel_id=4, replica_groups=mesh['dp'=8,'tensor'=32] {'tensor'}, dimensions={0}, use_global_device_ids=true | all-gather | bytes 270336 | tf_op jit(solution)/shard_map/all_gather | solution.py:10
  120.6 22.6 %all-gather = f32[65536]{0:T(1024)S(1)} all-gather(f32[2048]{0:T(1024)S(1)} %get-tuple-element.87), channel_id=2, replica_groups=mesh['dp'=8,'tensor'=32] {'tensor'}, dimensions={0}, use_global_device_ids=true | all-gather | bytes 270336 | tf_op jit(solution)/shard_map/all_gather | solution.py:10
  143.2 24.1 %all-gather.1 = f32[65536]{0:T(1024)S(1)} all-gather(f32[2048]{0:T(1024)S(1)} %get-tuple-element.59), channel_id=3, replica_groups=mesh['dp'=8,'tensor'=32] {'tensor'}, dimensions={0}, use_global_device_ids=true | all-gather | bytes 270336 | tf_op jit(solution)/shard_map/all_gather | solution.py:10
  167.3 22.6 %all-gather.3 = f32[65536]{0:T(1024)S(1)} all-gather(f32[2048]{0:T(1024)S(1)} %get-tuple-element.60), channel_id=5, replica_groups=mesh['dp'=8,'tensor'=32] {'tensor'}, dimensions={0}, use_global_device_ids=true | all-gather | bytes 270336 | tf_op jit(solution)/shard_map/all_gather | solution.py:10
  190.1 4.3 %while.16 = (s32[]{:T(128)}, f32[2048]{0:T(1024)S(1)}, f32[2048]{0:T(1024)S(1)}, f32[2048]{0:T(1024)S(1)}, f32[2048]{0:T(1024)S(1)}, /*index=5*/f32[31,2048]{1,0...) while((s32[]{:T(128)}, f32[2048]{0:T(1024)S(1)}, ...), condition=%wide.region_6.7_spmd, body=%wide.region_5.6_spmd.sunk | while | flops 32770 | bytes 221301 | solution.py:13
  194.4 0.0 copy-done
  194.4 0.6 subtract_multiply_fusion
  195.0 0.0 copy-start.1
  195.0 0.1 select_reduce_fusion.2
  195.1 0.0 copy-done.2
  195.2 0.0 copy-done.3
  195.2 0.1 select_reduce_fusion.1
  195.3 13.8 %psum.14 = f32[64]{0:T(128)S(1)} all-reduce(f32[64]{0:T(128)S(1)} %select_reduce_fusion.1), channel_id=1, replica_groups=mesh['dp'=8,'tensor'=32] {'dp'}, use_global_device_ids=true, to_apply=%region_11.12 | all-reduce | flops 64 | bytes 512 | tf_op jit(solution)/shard_map/psum | solution.py:72
  209.0 65.8 %psum.15 = f32[64]{0:T(128)S(1)} all-reduce(f32[64]{0:T(128)S(1)} %psum.14), channel_id=1, replica_groups=mesh['dp'=8,'tensor'=32] {'tensor'}, use_global_device_ids=true, to_apply=%region_12.13 | all-reduce | flops 64 | bytes 512 | tf_op jit(solution)/shard_map/psum | solution.py:72
  274.9 0.6 dynamic_slice.32
  275.5 0.0 copy-done.1
  (203 shorter events, 2.7 us)
Async XLA Ops:
  7.2 65.7 %all-gather.6.cloned.1.call-start = ((), (), s32[]{:S(2)}) async-start(), calls=%async_computation | async-start | bytes 8650752 | tf_op jit(solution)/shard_map/all_gather | solution.py:41
  91.3 103.1 %copy-start = (s32[64]{0:T(128)S(1)}, s32[64]{0:T(128)}, u32[]{:S(2)}) copy-start(s32[64]{0:T(128)} %param.15) | copy-start | bytes 772
  91.3 103.8 %copy-start.2 = (s32[1,8]{1,0:T(1,128)S(1)}, s32[1,8]{1,0:T(1,128)}, u32[]{:S(2)}) copy-start(s32[1,8]{1,0:T(1,128)} %param.16) | copy-start | bytes 100
  91.3 103.8 %copy-start.3 = (s32[8]{0:T(128)S(1)}, s32[8]{0:T(128)}, u32[]{:S(2)}) copy-start(s32[8]{0:T(128)} %param.17) | copy-start | bytes 100
  195.0 80.4 %copy-start.1 = (f32[64]{0:T(128)}, f32[64]{0:T(128)S(1)}, u32[]{:S(2)}) copy-start(f32[64]{0:T(128)S(1)} %get-tuple-element.86) | copy-start | bytes 772
Sparse Core Ops, SparseCore 0:
  10.6 62.2 all-gather.5

commit v2 on v0

--- a/solution.py
+++ b/solution.py
@@ -69,7 +69,7 @@
     all_requests = request_count * lax.axis_size("dp")
     route_table = request_order[:, None] == jnp.arange(all_requests, dtype=jnp.int32)[None, :]
     by_request = jnp.sum(jnp.where(route_table, by_pos[:, None], 0.0), axis=0)
-    totals = lax.psum(by_request, ("dp", "tensor"))
+    totals = jnp.sum(lax.all_gather(by_request, ("dp", "tensor")), axis=0)
     request_score = lax.dynamic_slice_in_dim(
         totals, lax.axis_index("dp") * request_count, request_count
     )

time: 279 us -> 442 us (1.58)
  waiting for transfers between devices: 42 us -> 280 us
  blocking collectives: 184 us -> 109 us
    unnamed x1 -> x3, waiting for transfers between devices: 0.02 us -> 236 us
    psum x1 -> x0, blocking collectives: 75.4 us -> none  [on_device(): totals = lax.psum(by_request, ('dp', 'tensor'))]
  transfers between devices with their start and end apart: 1 -> 2, of which waited for: 1 -> 2; matrix products, arithmetic and copies ran while one was open for 2% -> 1% of each run, Pallas kernels for 0% -> 0%
where the time goes in v2:
time: 442 us
  waiting for transfers between devices  280 us (63%)
  blocking collectives  109 us (25%)
  matrix products  19.1 us (4%)
  between operations  14.9 us (3%)
  other arithmetic  10.4 us (2%)
  local copies, waits for them, and re-layouts  6.94 us (2%)
    unnamed x3, waiting for transfers between devices  236 us
    all_gather x4, blocking collectives, merged_2(): pieces = jax.tree.map(lambda part: lax.all_gather(part, axis), value)  93.9 us
    all_gather x1, waiting for transfers between devices, on_device(): piece_rows = lax.all_gather(normed, 'tensor', axis=0, tiled=True)  43.5 us
    dot_general x1, matrix products, on_device(): jnp.dot(piece_rows, head_weight, preferred_element_type=jnp.float32)  18.4 us
    unnamed x1, blocking collectives  14.7 us
  transfers between devices with their start and end apart: 2, of which 2 were waited for; matrix products, arithmetic and copies ran while one was open for 1% of the time, Pallas kernels for 0%

profile of v2, /device:TPU:1, one launch (start us, length us, event | category | flops | bytes accessed | tf_op | source)
XLA Modules:
  0.0 441.7 jit_solution(12960260263963013514)
XLA Ops:
  7.2 0.0 all-gather.7.cloned.1.call-start
  7.2 1.1 fusion.2
  8.3 1.8 fusion.4
  10.1 0.0 all-gather.7.cloned.1.call-update
  10.2 0.0 all-reduce.4.cloned.1.call-start
  10.2 1.3 dynamic-slice
  11.5 0.8 reduce-window.8
  12.3 0.7 reshape.89
  13.7 0.9 dynamic-update-slice
  14.5 14.7 %all-reduce = s32[2048]{0:T(1024)S(1)} all-reduce(s32[2048]{0:T(1024)S(1)} %dynamic-update-slice), channel_id=1, replica_groups=mesh['dp'=8,'tensor'=32] {'tensor'}, use_global_device_ids=true, to_apply=%add | all-reduce | flops 2048 | bytes 16384
  29.3 0.1 convert_reduce_fusion
  29.3 43.5 %all-gather.7.cloned.1.call-done = bf16[2048,2048]{1,0:T(8,128)(2,1)} async-done(((bf16[64,2048]{1,0:T(8,128)(2,1)}), bf16[2048,2048]{1,0:T(8,128)(2,1)}) %all-gather.7.cloned.1.call-update) | async-done | bytes 8388624 | tf_op jit(solution)/shard_map/all_gather | solution.py:41
  72.9 18.4 %fusion.5 = (f32[2048]{0:T(1024)S(1)}, f32[2048,1572]{0,1:T(8,128)S(1)}) fusion(bf16[2048,2048]{1,0:T(8,128)(2,1)} %all-gather.7.cloned.1.call-done, bf16[2048,1572]{0,1:T(8,128)(2,1)} %param.12), kind=kOutput, calls=%fused_computation.28 | convolution fusion | flops 13190109184 | bytes 27713536 | tf_op jit(solution)/shard_map/dot_general | solution.py:43
  91.3 0.0 copy-start.2
  91.3 0.0 copy-start.4
  91.3 0.0 copy-start.5
  91.3 0.0 copy-start
  91.3 4.7 %fusion = (f32[2048]{0:T(1024)S(1)}, f32[2048]{0:T(1024)S(1)}, f32[2048]{0:T(1024)S(1)}) fusion(f32[2048,1572]{0,1:T(8,128)S(1)} %get-tuple-element.88, f32[2048]{0:T(1024)S(1)} %get-tuple-element.87, s32[2048]{0:T(1024)S(1)} %all-reduce, s32[1572]{0:T(1024)S(1)} %iota_add_fusion), kind=kLoop, calls=%fused_computation.8 | loop fusion | flops 22530048 | bytes 12925072 | tf_op jit(solution)/shard_map/reduce_sum | solution.py:48
  96.1 24.5 %all-gather.2 = f32[65536]{0:T(1024)S(1)} all-gather(f32[2048]{0:T(1024)S(1)} %get-tuple-element.58), channel_id=4, replica_groups=mesh['dp'=8,'tensor'=32] {'tensor'}, dimensions={0}, use_global_device_ids=true | all-gather | bytes 270336 | tf_op jit(solution)/shard_map/all_gather | solution.py:10
  120.6 22.6 %all-gather = f32[65536]{0:T(1024)S(1)} all-gather(f32[2048]{0:T(1024)S(1)} %get-tuple-element.87), channel_id=2, replica_groups=mesh['dp'=8,'tensor'=32] {'tensor'}, dimensions={0}, use_global_device_ids=true | all-gather | bytes 270336 | tf_op jit(solution)/shard_map/all_gather | solution.py:10
  143.2 24.1 %all-gather.1 = f32[65536]{0:T(1024)S(1)} all-gather(f32[2048]{0:T(1024)S(1)} %get-tuple-element.59), channel_id=3, replica_groups=mesh['dp'=8,'tensor'=32] {'tensor'}, dimensions={0}, use_global_device_ids=true | all-gather | bytes 270336 | tf_op jit(solution)/shard_map/all_gather | solution.py:10
  167.4 22.8 %all-gather.3 = f32[65536]{0:T(1024)S(1)} all-gather(f32[2048]{0:T(1024)S(1)} %get-tuple-element.60), channel_id=5, replica_groups=mesh['dp'=8,'tensor'=32] {'tensor'}, dimensions={0}, use_global_device_ids=true | all-gather | bytes 270336 | tf_op jit(solution)/shard_map/all_gather | solution.py:10
  190.3 4.3 while.16
  194.6 0.0 copy-done.2
  194.6 0.6 subtract_multiply_fusion
  195.2 0.0 copy-start.3
  195.2 0.1 select_reduce_fusion.2
  195.3 0.0 copy-done.4
  195.3 0.0 copy-done.5
  195.4 0.1 select_reduce_fusion.1
  195.4 0.3 dynamic-update-slice.1
  195.7 0.0 copy-start.1
  195.7 0.6 copy-done.1
  196.3 0.0 all-reduce.4.cloned.1.call-update
  196.4 0.0 copy-done
  196.4 0.7 fusion.1
  197.1 236.2 %all-reduce.4.cloned.1.call-done = f32[16384]{0:T(1024)} async-done(((f32[16384]{0:T(1024)}), f32[16384]{0:T(1024)}) %all-reduce.4.cloned.1.call-update) | async-done | bytes 65552
  433.3 0.9 reshape.69
  434.2 0.1 reduce_sum.79
  434.3 0.6 dynamic_slice.32
  434.9 0.0 copy-done.3
  (204 shorter events, 2.7 us)
Async XLA Ops:
  7.2 65.7 %all-gather.7.cloned.1.call-start = ((), (), s32[]{:S(2)}) async-start(), calls=%async_computation | async-start | bytes 8650752 | tf_op jit(solution)/shard_map/all_gather | solution.py:41
  10.2 423.1 %all-reduce.4.cloned.1.call-start = ((), (), s32[]{:S(2)}) async-start(), calls=%async_computation.1 | async-start | bytes 131072
  91.3 103.3 %copy-start.2 = (s32[64]{0:T(128)S(1)}, s32[64]{0:T(128)}, u32[]{:S(2)}) copy-start(s32[64]{0:T(128)} %param.15) | copy-start | bytes 772
  91.3 104.0 %copy-start.4 = (s32[1,8]{1,0:T(1,128)S(1)}, s32[1,8]{1,0:T(1,128)}, u32[]{:S(2)}) copy-start(s32[1,8]{1,0:T(1,128)} %param.16) | copy-start | bytes 100
  91.3 104.0 %copy-start.5 = (s32[8]{0:T(128)S(1)}, s32[8]{0:T(128)}, u32[]{:S(2)}) copy-start(s32[8]{0:T(128)} %param.17) | copy-start | bytes 100
  91.3 105.0 %copy-start = (bf16[64,2048]{1,0:T(8,128)(2,1)S(1)}, bf16[64,2048]{1,0:T(8,128)(2,1)}, u32[]{:S(2)}) copy-start(bf16[64,2048]{1,0:T(8,128)(2,1)} %fusion.4) | copy-start | bytes 786436
  195.2 239.7 %copy-start.3 = (f32[64]{0:T(128)}, f32[64]{0:T(128)S(1)}, u32[]{:S(2)}) copy-start(f32[64]{0:T(128)S(1)} %get-tuple-element.86) | copy-start | bytes 772
  195.7 0.6 copy-start.1
Sparse Core Ops, SparseCore 0:
  10.6 62.2 all-gather.6
  196.5 236.7 all-reduce.3
